TPU v7x, 32 devices: a whole 2x2x4 slice. The times are simulated.
32 devices in a mesh: grp: 4 (over z), fsdp: 8 (over y, x, core).
Axes of the slice: x: 2, y: 2, z: 4, core: 2. Of those that a mesh axis runs over, the one named last changes fastest.
Arguments:
- acts: bfloat16 [64, 128, 4096], P(('grp', 'fsdp'))
- out_grads: bfloat16 [64, 128, 1024], P(('grp', 'fsdp'))
- doc_lengths: int32 [64], P(('grp', 'fsdp')), may hold values from 32 to 128
- proj_in: bfloat16 [64, 4096], replicated, may hold values from -0.09375 to 0.09375
- proj_out: bfloat16 [64, 1024], replicated, may hold values from -0.1875 to 0.1875
- store_grads: bfloat16 [7168, 4096], P(('grp', 'fsdp')), may hold values from -6 to 6
- queries: bfloat16 [512, 4096], P('fsdp'), may hold values from -6 to 6
Outputs:
- new_grads: bfloat16 [64, 4096], P(('grp', 'fsdp'))
- store_scores: bfloat16 [7168, 512], P(('grp', 'fsdp'))
- new_scores: bfloat16 [64, 512], P(('grp', 'fsdp'))
All inputs are finite; a program needn't handle non-finite values.
Results may differ from a plain program's by a relative error of at most 0.012.
The roundings to bfloat16 on the way count: a program that leaves them out, or rounds other values in their place, can miss the bound.
Values may be sent and summed in bfloat16 or wider, within the bound.
A program may use at most 64 MiB of HBM per device.

v0:
```python
import jax
import jax.numpy as jnp
from jax import lax
from jax.sharding import PartitionSpec as P


def damped_inverse(summed, token_count, identity_matrix):
    proj_rank = identity_matrix.shape[0]
    covariance = summed / token_count
    damped = covariance + 0.1 * jnp.trace(covariance) / proj_rank * identity_matrix
    lower_factor = jnp.linalg.cholesky(damped)
    return jax.scipy.linalg.cho_solve((lower_factor, True), identity_matrix)


def precondition(query_rows, out_inverse, in_inverse):
    proj_rank = out_inverse.shape[0]
    query_mats = query_rows.astype(jnp.float32).reshape(query_rows.shape[0], proj_rank, proj_rank)
    half_done = jnp.einsum("ab,qbc->qac", out_inverse, query_mats, precision=lax.Precision.HIGHEST)
    precond = jnp.einsum("qac,cd->qad", half_done, in_inverse, precision=lax.Precision.HIGHEST)
    return precond.reshape(query_rows.shape[0], proj_rank * proj_rank).astype(jnp.bfloat16)


def project(tokens, projection):
    docs_here, length, features = tokens.shape
    flat = tokens.reshape(docs_here * length, features)
    result = lax.dot_general(
        flat, projection, (((1,), (1,)), ((), ())), preferred_element_type=jnp.float32
    )
    return result.reshape(docs_here, length, projection.shape[0])


def factor_totals(in_factor, out_factor, token_count):
    return lax.psum((in_factor, out_factor, token_count), ("grp", "fsdp"))


def shards(acts, out_grads, doc_lengths, proj_in, proj_out, store_grads, queries):
    docs_here, length, features = acts.shape
    proj_rank = proj_in.shape[0]
    identity_matrix = jnp.eye(proj_rank, dtype=jnp.float32)
    positions = lax.broadcasted_iota(jnp.int32, (docs_here, length), 1)
    valid_mask = (positions < doc_lengths[:, None]).astype(jnp.float32)
    in_proj = project(acts, proj_in)
    out_proj = project(out_grads, proj_out)
    in_masked = in_proj * valid_mask[:, :, None]
    out_masked = out_proj * valid_mask[:, :, None]
    in_factor = jnp.einsum("dta,dtb->ab", in_masked, in_proj, precision=lax.Precision.HIGHEST)
    out_factor = jnp.einsum("dta,dtb->ab", out_masked, out_proj, precision=lax.Precision.HIGHEST)
    token_count = jnp.sum(valid_mask)
    per_doc = jnp.einsum("dta,dtb->dab", out_masked, in_proj, precision=lax.Precision.HIGHEST)
    per_doc = per_doc / doc_lengths.astype(jnp.float32)[:, None, None]
    new_grads = per_doc.reshape(docs_here, proj_rank * proj_rank).astype(jnp.bfloat16)
    score_rows = jnp.concatenate([store_grads, new_grads], axis=0)
    stored = store_grads.shape[0]
    in_total, out_total, tokens_total = factor_totals(in_factor, out_factor, token_count)
    in_inverse = damped_inverse(in_total, tokens_total, identity_matrix)
    out_inverse = damped_inverse(out_total, tokens_total, identity_matrix)
    prepared_local = precondition(queries, out_inverse, in_inverse)
    scores = lax.dot_general(
        score_rows,
        lax.all_gather(prepared_local, "fsdp", axis=0, tiled=True),
        (((1,), (1,)), ((), ())),
        preferred_element_type=jnp.float32,
    )
    store_scores = scores[:stored].astype(jnp.bfloat16)
    new_scores = scores[stored:].astype(jnp.bfloat16)
    return (new_grads, store_scores, new_scores)


def solution(mesh):
    placed = (
        P(("grp", "fsdp"), None, None),
        P(("grp", "fsdp"), None, None),
        P(("grp", "fsdp")),
        P(),
        P(),
        P(("grp", "fsdp"), None),
        P("fsdp", None),
    )
    return jax.shard_map(
        shards,
        mesh=mesh,
        in_specs=placed,
        out_specs=(P(("grp", "fsdp"), None), P(("grp", "fsdp"), None), P(("grp", "fsdp"), None)),
        check_vma=False,
    )
```

profile of v0, /device:TPU:0, one launch (start us, length us, event | category | flops | bytes accessed | tf_op | source)
XLA Modules:
  0.0 139.9 jit_solution(4176288750345755124)
XLA Ops:
  7.2 1.5 %fusion.36 = f32[]{:T(128)} fusion(s32[2]{0:T(128)} %param.12), kind=kLoop, calls=%fused_computation.55 | loop fusion | flops 767 | bytes 12 | tf_op jit(solution)/shard_map/reduce_sum | solution.py:48
  8.7 0.7 compare_convert_fusion
  9.5 1.8 %fusion.13 = f32[2,128,64]{1,2,0:T(8,128)S(1)} fusion(bf16[2,128,4096]{2,1,0:T(8,128)(2,1)S(1)} %copy-done, bf16[64,4096]{1,0:T(8,128)(2,1)} %param.13), kind=kOutput, calls=%fused_computation.14 | convolution fusion | flops 134217728 | bytes 2686976 | tf_op jit(solution)/shard_map/dot_general | solution.py:26
  11.3 0.2 convolution_bitcast_fusion.1
  11.5 0.3 fusion.15
  11.8 0.2 convolution_bitcast_fusion.3
  12.0 42.9 %all-reduce = (f32[64,64]{0,1:T(8,128)S(1)}, f32[]{:T(128)}, f32[64,64]{0,1:T(8,128)S(1)}) all-reduce(f32[64,64]{0,1:T(8,128)S(1)} %convolution_bitcast_fusion.1, f32[]{:T(128)} %fusion.36, f32[64,64]{0,1:T(8,128)S(1)} %convolution_bitcast_fusion.3), channel_id=1, replica_groups=mesh['grp'=4,'fsdp'=8] {'grp','fsdp'}, use_global_device_ids=true, to_apply=%region_6.9 | all-reduce | flops 8193 | bytes 65544 | tf_op jit(solution)/shard_map/psum | solution.py:33
  54.9 1.3 select_reduce_fusion.3
  56.1 1.3 select_reduce_fusion.2
  58.7 0.7 select_add_fusion
  59.5 5.8 %cholesky.55 = f32[64,64]{1,0:T(8,128)S(1)} custom-call(f32[64,64]{1,0:T(8,128)S(1)} %fusion.28), custom_call_target="Cholesky" | custom-call | tf_op jit(solution)/shard_map/jit(cholesky)/cholesky | solution.py:11
  65.4 0.6 compare_reduce_fusion
  66.0 0.7 fusion.25
  66.7 4.9 %custom-call.9 = f32[1,64,64]{1,2,0:T(8,128)S(1)} custom-call(f32[1,64,64]{2,1,0:T(8,128)S(1)} %fusion.25), custom_call_target="InvertDiagBlocksLowerTriangular" | custom-call | tf_op jit(solution)/shard_map/jit(_cho_solve)/triangular_solve | solution.py:12
  71.6 0.3 fusion.20
  71.8 0.2 convolution_bitcast_fusion
  72.1 5.8 %cholesky.44 = f32[64,64]{1,0:T(8,128)S(1)} custom-call(f32[64,64]{1,0:T(8,128)S(1)} %fusion.31), custom_call_target="Cholesky" | custom-call | tf_op jit(solution)/shard_map/jit(cholesky)/cholesky | solution.py:11
  78.0 0.6 compare_reduce_fusion.1
  78.6 0.7 fusion.24
  79.3 4.9 %custom-call.8 = f32[1,64,64]{1,2,0:T(8,128)S(1)} custom-call(f32[1,64,64]{2,1,0:T(8,128)S(1)} %fusion.24), custom_call_target="InvertDiagBlocksLowerTriangular" | custom-call | tf_op jit(solution)/shard_map/jit(_cho_solve)/triangular_solve | solution.py:12
  84.2 0.3 fusion.22
  84.4 0.2 convolution_bitcast_fusion.2
  84.6 2.1 %reshape.52 = bf16[64,64,64]{2,1,0:T(8,128)(2,1)S(1)} reshape(bf16[64,4096]{1,0:T(8,128)(2,1)} %param.16) | data formatting | bytes 1048576 | tf_op jit(solution)/shard_map/reshape | solution.py:17
  86.7 1.0 fusion.37
  87.7 1.8 %fusion.6 = bf16[64,64,64]{2,1,0:T(8,128)(2,1)S(1)} fusion(f32[64,64,1]{1,0,2:T(8,128)S(1)} %convolution_bitcast_fusion, f32[64,64,64]{2,0,1:T(8,128)S(1)} %fusion.37), kind=kOutput, calls=%fused_computation.6 | convolution fusion | flops 201588736 | bytes 1589248 | tf_op jit(solution)/shard_map/qac,cd->qad/dot_general | solution.py:19
  89.4 1.6 %convert_element_type.36 = bf16[64,4096]{1,0:T(8,128)(2,1)} reshape(bf16[64,64,64]{2,1,0:T(8,128)(2,1)S(1)} %fusion.6) | data formatting | bytes 1048576 | tf_op jit(solution)/shard_map/convert_element_type | solution.py:20
  91.1 0.2 fusion.12
  91.3 0.1 convert_element_type.33
  91.5 36.3 %all-gather.2.cloned.1.call-done = bf16[512,4096]{1,0:T(8,128)(2,1)} async-done(((bf16[64,4096]{1,0:T(8,128)(2,1)}), bf16[512,4096]{1,0:T(8,128)(2,1)}) %all-gather.2.cloned.1.call-update) | async-done | bytes 4194320 | tf_op jit(solution)/shard_map/all_gather | solution.py:60
  127.8 4.0 %fusion.9 = bf16[226,512]{1,0:T(8,128)(2,1)S(1)} fusion(bf16[512,4096]{1,0:T(8,128)(2,1)} %all-gather.2.cloned.1.call-done, bf16[2,4096]{1,0:T(2,128)(2,1)S(1)} %convert_element_type.33, bf16[224,4096]{1,0:T(8,128)(2,1)} %param.15), kind=kOutput, calls=%fused_computation.7 | convolution fusion | flops 951731200 | bytes 6277120 | tf_op jit(solution)/shard_map/dot_general | solution.py:58
  131.8 0.6 slice.23
  132.4 0.7 slice.22
  (19 shorter events, 0.3 us)
Async XLA Ops:
  7.2 2.3 %copy-start = (bf16[2,128,4096]{2,1,0:T(8,128)(2,1)S(1)}, bf16[2,128,4096]{2,1,0:T(8,128)(2,1)}, u32[]{:S(2)}) copy-start(bf16[2,128,4096]{2,1,0:T(8,128)(2,1)} %param.10) | copy-start | bytes 6291460
  7.2 4.3 %copy-start.2 = (bf16[64,1024]{1,0:T(8,128)(2,1)S(1)}, bf16[64,1024]{1,0:T(8,128)(2,1)}, u32[]{:S(2)}) copy-start(bf16[64,1024]{1,0:T(8,128)(2,1)} %param.14) | copy-start | bytes 393220
  7.2 4.3 %copy-start.1 = (bf16[2,128,1024]{2,1,0:T(8,128)(2,1)S(1)}, bf16[2,128,1024]{2,1,0:T(8,128)(2,1)}, u32[]{:S(2)}) copy-start(bf16[2,128,1024]{2,1,0:T(8,128)(2,1)} %param.11) | copy-start | bytes 1572868
  7.2 120.6 %all-gather.2.cloned.1.call-start = ((), (), s32[]{:S(2)}) async-start(), calls=%async_computation | async-start | bytes 4718592 | tf_op jit(solution)/shard_map/all_gather | solution.py:60
  87.6 3.4 %copy-start.4 = (s32[2]{0:T(128)S(1)}, s32[2]{0:T(128)}, u32[]{:S(2)}) copy-start(s32[2]{0:T(128)} %param.12) | copy-start | bytes 28
  91.4 40.4 %copy-start.3 = (bf16[2,4096]{1,0:T(2,128)(2,1)}, bf16[2,4096]{1,0:T(2,128)(2,1)S(1)}, u32[]{:S(2)}) copy-start(bf16[2,4096]{1,0:T(2,128)(2,1)S(1)} %convert_element_type.33) | copy-start | bytes 49156
Sparse Core Ops, SparseCore 0:
  91.2 36.5 all-gather.1
where the time goes:
time: 140 us
  blocking collectives  42.9 us (31%)
  waiting for transfers between devices  36.3 us (26%)
  other arithmetic  29.5 us (21%)
  between operations  15.6 us (11%)
  matrix products  10.3 us (7%)
  local copies, waits for them, and re-layouts  5.25 us (4%)
    psum x1, blocking collectives, factor_totals(): return lax.psum((in_factor, out_factor, token_count), ('grp', 'fsdp'))  42.9 us
    all_gather x1, waiting for transfers between devices, shards(): lax.all_gather(prepared_local, 'fsdp', axis=0, tiled=True)  36.3 us
    another operation x6, other arithmetic, damped_inverse(): lower_factor = jnp.linalg.cholesky(damped)  13 us
    another operation x4, other arithmetic, damped_inverse(): return jax.scipy.linalg.cho_solve((lower_factor, True), identity_matrix)  11.1 us
    dot_general x1, matrix products, shards(): lax.dot_general(score_rows, lax.all_gather(prepared_local, 'fsdp', axis=0...  4.03 us
  transfers between devices with their start and end apart: 1, of which 1 were waited for; matrix products, arithmetic and copies ran while one was open for 0% of the time, Pallas kernels for 0%

commit v1 on v0

--- a/solution.py
+++ b/solution.py
@@ -2,6 +2,28 @@
 import jax.numpy as jnp
 from jax import lax
 from jax.sharding import PartitionSpec as P
+
+
+def in_order(blocks, dim):
+    blocks = jnp.moveaxis(blocks, 0, dim)
+    shape = blocks.shape
+    return blocks.reshape(*shape[:dim], shape[dim] * shape[dim + 1], *shape[dim + 2 :])
+
+
+def doubled(shard, axis):
+    size = lax.axis_size(axis)
+    blocks = shard[None]
+    for level in range(size.bit_length() - 1):
+        apart = 1 << level
+        other = lax.ppermute(blocks, axis, [(i, i ^ apart) for i in range(size)])
+        both = jnp.stack([blocks, other])
+        upper = lax.axis_index(axis) >> level & 1
+        blocks = jnp.where(upper == 0, both, both[::-1]).reshape(-1, *shard.shape)
+    return blocks
+
+
+def collect(array, axis, dim):
+    return in_order(doubled(array, axis), dim)
 
 
 def damped_inverse(summed, token_count, identity_matrix):
@@ -57,7 +79,7 @@
     prepared_local = precondition(queries, out_inverse, in_inverse)
     scores = lax.dot_general(
         score_rows,
-        lax.all_gather(prepared_local, "fsdp", axis=0, tiled=True),
+        collect(prepared_local, "fsdp", 0),
         (((1,), (1,)), ((), ())),
         preferred_element_type=jnp.float32,
     )

time: 140 us -> 173 us (1.24)
  waiting for transfers between devices: 36.3 us -> 69.8 us
  between operations: 15.6 us -> 2.18 us
  other arithmetic: 29.5 us -> 39.1 us
  starting transfers between devices: 0.04 us -> 4.01 us
  matrix products: 10.3 us -> 7.61 us
  local copies, waits for them, and re-layouts: 5.25 us -> 7.38 us
    ppermute x0 -> x3, waiting for transfers between devices: none -> 69.8 us  [doubled(): other = lax.ppermute(blocks, axis, [(i, i ^ apart) for i in range(size)])]
    all_gather x1 -> x0, waiting for transfers between devices: 36.3 us -> none  [shards(): lax.all_gather(prepared_local, 'fsdp', axis=0, tiled=True)]
    another operation x0 -> x4, other arithmetic: none -> 6.61 us  [doubled(): both = jnp.stack([blocks, other])]
    ppermute x0 -> x3, starting transfers between devices: none -> 4.01 us  [doubled(): other = lax.ppermute(blocks, axis, [(i, i ^ apart) for i in range(size)])]
    select_n x0 -> x2, other arithmetic: none -> 2.96 us  [doubled(): blocks = jnp.where(upper == 0, both, both[::-1]).reshape(-1, *shard.shape)]
    dot_general x1, matrix products: 4.03 us -> 1.29 us  [shards(): lax.dot_general(score_rows, collect(prepared_local, 'fsdp', 0), (((1,), (...]
  transfers between devices with their start and end apart: 1 -> 3, of which waited for: 1 -> 3; matrix products, arithmetic and copies ran while one was open for 0% -> 1% of each run, Pallas kernels for 0% -> 0%
where the time goes in v1:
time: 173 us
  waiting for transfers between devices  69.8 us (40%)
  blocking collectives  42.9 us (25%)
  other arithmetic  39.1 us (23%)
  matrix products  7.61 us (4%)
  local copies, waits for them, and re-layouts  7.38 us (4%)
  starting transfers between devices  4.01 us (2%)
  between operations  2.18 us (1%)
    ppermute x3, waiting for transfers between devices, doubled(): other = lax.ppermute(blocks, axis, [(i, i ^ apart) for i in range(size)])  69.8 us
    psum x1, blocking collectives, factor_totals(): return lax.psum((in_factor, out_factor, token_count), ('grp', 'fsdp'))  42.9 us
    another operation x6, other arithmetic, damped_inverse(): lower_factor = jnp.linalg.cholesky(damped)  13 us
    another operation x4, other arithmetic, damped_inverse(): return jax.scipy.linalg.cho_solve((lower_factor, True), identity_matrix)  11.1 us
    another operation x4, other arithmetic, doubled(): both = jnp.stack([blocks, other])  6.61 us
    ppermute x3, starting transfers between devices, doubled(): other = lax.ppermute(blocks, axis, [(i, i ^ apart) for i in range(size)])  4.01 us
  transfers between devices with their start and end apart: 3, of which 3 were waited for; matrix products, arithmetic and copies ran while one was open for 1% of the time, Pallas kernels for 0%

profile of v1, /device:TPU:0, one launch (start us, length us, event | category | flops | bytes accessed | tf_op | source)
XLA Modules:
  0.0 172.9 jit_solution(6468890517854114027)
XLA Ops:
  0.7 1.5 fusion.38
  2.1 0.7 compare_convert_fusion
  2.9 1.8 %fusion.15 = f32[2,128,64]{1,2,0:T(8,128)S(1)} fusion(bf16[2,128,4096]{2,1,0:T(8,128)(2,1)S(1)} %copy-done, bf16[64,4096]{1,0:T(8,128)(2,1)} %param.13), kind=kOutput, calls=%fused_computation.22 | convolution fusion | flops 134217728 | bytes 2686976 | tf_op jit(solution)/shard_map/dot_general | solution.py:48
  5.4 42.9 %all-reduce = (f32[64,64]{0,1:T(8,128)S(1)}, f32[]{:T(128)}, f32[64,64]{0,1:T(8,128)S(1)}) all-reduce(f32[64,64]{0,1:T(8,128)S(1)} %convolution_bitcast_fusion.1, f32[]{:T(128)} %fusion.38, f32[64,64]{0,1:T(8,128)S(1)} %convolution_bitcast_fusion.3), channel_id=1, replica_groups=mesh['grp'=4,'fsdp'=8] {'grp','fsdp'}, use_global_device_ids=true, to_apply=%region_6.9 | all-reduce | flops 8193 | bytes 65544 | tf_op jit(solution)/shard_map/psum | solution.py:55
  48.3 1.3 select_reduce_fusion.3
  49.6 1.3 select_reduce_fusion.2
  52.1 0.7 select_add_fusion
  52.9 5.8 %cholesky.55 = f32[64,64]{1,0:T(8,128)S(1)} custom-call(f32[64,64]{1,0:T(8,128)S(1)} %fusion.30), custom_call_target="Cholesky" | custom-call | tf_op jit(solution)/shard_map/jit(cholesky)/cholesky | solution.py:33
  58.8 0.6 compare_reduce_fusion
  59.4 0.7 fusion.27
  60.1 4.9 %custom-call.9 = f32[1,64,64]{1,2,0:T(8,128)S(1)} custom-call(f32[1,64,64]{2,1,0:T(8,128)S(1)} %fusion.27), custom_call_target="InvertDiagBlocksLowerTriangular" | custom-call | tf_op jit(solution)/shard_map/jit(_cho_solve)/triangular_solve | solution.py:34
  65.5 5.8 %cholesky.44 = f32[64,64]{1,0:T(8,128)S(1)} custom-call(f32[64,64]{1,0:T(8,128)S(1)} %fusion.33), custom_call_target="Cholesky" | custom-call | tf_op jit(solution)/shard_map/jit(cholesky)/cholesky | solution.py:33
  71.4 0.6 compare_reduce_fusion.1
  72.0 0.7 fusion.26
  72.7 4.9 %custom-call.8 = f32[1,64,64]{1,2,0:T(8,128)S(1)} custom-call(f32[1,64,64]{2,1,0:T(8,128)S(1)} %fusion.26), custom_call_target="InvertDiagBlocksLowerTriangular" | custom-call | tf_op jit(solution)/shard_map/jit(_cho_solve)/triangular_solve | solution.py:34
  78.0 2.2 %reshape.79 = bf16[64,64,64]{2,1,0:T(8,128)(2,1)S(1)} reshape(bf16[64,4096]{1,0:T(8,128)(2,1)} %param.16) | data formatting | bytes 1048576 | tf_op jit(solution)/shard_map/reshape | solution.py:39
  80.2 1.0 fusion.39
  81.2 1.8 %fusion.6 = bf16[64,64,64]{2,1,0:T(8,128)(2,1)S(1)} fusion(f32[64,64,1]{1,0,2:T(8,128)S(1)} %convolution_bitcast_fusion, f32[64,64,64]{2,0,1:T(8,128)S(1)} %fusion.39), kind=kOutput, calls=%fused_computation.11 | convolution fusion | flops 201588736 | bytes 1589248 | tf_op jit(solution)/shard_map/qac,cd->qad/dot_general | solution.py:41
  83.0 1.6 convert_element_type.54
  84.6 1.6 convert_element_type.53
  86.9 1.3 pad_maximum_fusion.2
  88.2 1.3 fusion.14
  89.5 2.3 %collective-permute-start.1 = (bf16[2,64,4096]{2,1,0:T(8,128)(2,1)}, bf16[2,64,4096]{2,1,0:T(8,128)(2,1)}, u32[]{:S(2)}, u32[]{:S(2)}) collective-permute-start(bf16[2,64,4096]{2,1,0:T(8,128)(2,1)} %get-tuple-element.9), channel_id=1, source_target_pairs={{0,2},{1,3},{2,0},{3,1},{4,6},{5,7},{6,4},{7,5},{8,10},{9,11},{10,... | collective-permute-start | bytes 3145736 | tf_op jit(solution)/shard_map/ppermute | solution.py:18
  91.7 23.8 %collective-permute-done.1 = bf16[2,64,4096]{2,1,0:T(8,128)(2,1)} collective-permute-done((bf16[2,64,4096]{2,1,0:T(8,128)(2,1)}, bf16[2,64,4096]{2,1,0:T(8,128)(2,1)}, u32[]{:S(2)}, u32[]{:S(2)}) %collective-permute-start.1) | collective-permute-done | bytes 1048608 | tf_op jit(solution)/shard_map/ppermute | solution.py:18
  115.5 1.4 pad_maximum_fusion.1
  116.9 1.8 %reverse_select_fusion.1 = bf16[2,2,64,4096]{3,2,1,0:T(8,128)(2,1)} fusion(bf16[2,2,64,4096]{3,2,1,0:T(8,128)(2,1)S(1)} %pad_maximum_fusion.1, pred[]{:T(512)S(6)} %eq.26), kind=kLoop, calls=%fused_computation.2 | loop fusion | flops 1048576 | bytes 4194305 | tf_op jit(solution)/shard_map/jit(_where)/select_n | solution.py:21
  118.8 1.7 %collective-permute-start.2 = (bf16[4,64,4096]{2,1,0:T(8,128)(2,1)}, bf16[4,64,4096]{2,1,0:T(8,128)(2,1)}, u32[]{:S(2)}, u32[]{:S(2)}) collective-permute-start(bf16[4,64,4096]{2,1,0:T(8,128)(2,1)} %bitcast.18), channel_id=1, source_target_pairs={{0,4},{1,5},{2,6},{3,7},{4,0},{5,1},{6,2},{7,3},{8,12},{9,13},{10,... | collective-permute-start | bytes 6291464 | tf_op jit(solution)/shard_map/ppermute | solution.py:18
  120.9 45.4 %collective-permute-done.2 = bf16[4,64,4096]{2,1,0:T(8,128)(2,1)} collective-permute-done((bf16[4,64,4096]{2,1,0:T(8,128)(2,1)}, bf16[4,64,4096]{2,1,0:T(8,128)(2,1)}, u32[]{:S(2)}, u32[]{:S(2)}) %collective-permute-start.2) | collective-permute-done | bytes 2097184 | tf_op jit(solution)/shard_map/ppermute | solution.py:18
  166.2 2.6 %pad_maximum_fusion = bf16[2,4,64,4096]{3,2,1,0:T(8,128)(2,1)S(1)} fusion(bf16[1,4,64,4096]{3,2,1,0:T(8,128)(2,1)} %bitcast.19, bf16[1,4,64,4096]{3,2,1,0:T(8,128)(2,1)} %bitcast.17), kind=kLoop, calls=%fused_computation.1 | loop fusion | flops 2097152 | bytes 8388608 | tf_op jit(solution)/shard_map/stack | solution.py:19
  168.9 1.1 reverse_select_fusion
  170.4 1.3 fusion.9
  172.2 0.7 slice.22
  (31 shorter events, 3.7 us)
Async XLA Ops:
  0.6 2.2 %copy-start = (bf16[2,128,4096]{2,1,0:T(8,128)(2,1)S(1)}, bf16[2,128,4096]{2,1,0:T(8,128)(2,1)}, u32[]{:S(2)}) copy-start(bf16[2,128,4096]{2,1,0:T(8,128)(2,1)} %param.10) | copy-start | bytes 6291460
  0.6 4.2 %copy-start.2 = (bf16[64,1024]{1,0:T(8,128)(2,1)S(1)}, bf16[64,1024]{1,0:T(8,128)(2,1)}, u32[]{:S(2)}) copy-start(bf16[64,1024]{1,0:T(8,128)(2,1)} %param.14) | copy-start | bytes 393220
  0.7 4.2 %copy-start.1 = (bf16[2,128,1024]{2,1,0:T(8,128)(2,1)S(1)}, bf16[2,128,1024]{2,1,0:T(8,128)(2,1)}, u32[]{:S(2)}) copy-start(bf16[2,128,1024]{2,1,0:T(8,128)(2,1)} %param.11) | copy-start | bytes 1572868
  84.6 2.3 %collective-permute-start = (bf16[1,64,4096]{2,1,0:T(8,128)(2,1)}, bf16[1,64,4096]{2,1,0:T(8,128)(2,1)}, u32[]{:S(2)}, u32[]{:S(2)}) collective-permute-start(bf16[1,64,4096]{2,1,0:T(8,128)(2,1)} %convert_element_type.54), channel_id=1, source_target_pairs={{0,1},{1,0},{2,3},{3,2},{4,5},{5,4},{6,7},{7,6},{8,9},{9,8},{10,11... | collective-permute-start | bytes 1572872 | tf_op jit(solution)/shard_map/ppermute | solution.py:18
  89.5 26.0 %collective-permute-start.1 = (bf16[2,64,4096]{2,1,0:T(8,128)(2,1)}, bf16[2,64,4096]{2,1,0:T(8,128)(2,1)}, u32[]{:S(2)}, u32[]{:S(2)}) collective-permute-start(bf16[2,64,4096]{2,1,0:T(8,128)(2,1)} %get-tuple-element.9), channel_id=1, source_target_pairs={{0,2},{1,3},{2,0},{3,1},{4,6},{5,7},{6,4},{7,5},{8,10},{9,11},{10,... | collective-permute-start | bytes 3145736 | tf_op jit(solution)/shard_map/ppermute | solution.py:18
  116.9 3.6 %copy-start.5 = (s32[2]{0:T(128)S(1)}, s32[2]{0:T(128)}, u32[]{:S(2)}) copy-start(s32[2]{0:T(128)} %param.12) | copy-start | bytes 28
  118.8 47.5 %collective-permute-start.2 = (bf16[4,64,4096]{2,1,0:T(8,128)(2,1)}, bf16[4,64,4096]{2,1,0:T(8,128)(2,1)}, u32[]{:S(2)}, u32[]{:S(2)}) collective-permute-start(bf16[4,64,4096]{2,1,0:T(8,128)(2,1)} %bitcast.18), channel_id=1, source_target_pairs={{0,4},{1,5},{2,6},{3,7},{4,0},{5,1},{6,2},{7,3},{8,12},{9,13},{10,... | collective-permute-start | bytes 6291464 | tf_op jit(solution)/shard_map/ppermute | solution.py:18
  120.9 49.2 %copy-start.3 = (bf16[2,4096]{1,0:T(2,128)(2,1)}, bf16[2,4096]{1,0:T(2,128)(2,1)S(1)}, u32[]{:S(2)}) copy-start(bf16[2,4096]{1,0:T(2,128)(2,1)S(1)} %convert_element_type.50) | copy-start | bytes 49156
  168.8 1.5 copy-start.4
